TPU v7x, 256 devices: a whole 4x4x8 slice. The times are simulated.
256 devices in a mesh: dp: 4 (over x), expert: 64 (over y, z, core).
Axes of the slice: x: 4, y: 4, z: 8, core: 2. Of those that a mesh axis runs over, the one named last changes fastest.
Arguments:
- frames: bfloat16 [32768, 1024], P(('dp', 'expert')), may hold values from -6 to 6
- lengths: int32 [256], P(('dp', 'expert')), may hold values from 64 to 128
- expert_ids: int32 [32768, 2], P(('dp', 'expert')), may hold values from 0 to 63, all different within a row
- conv_in: bfloat16 [1024, 2048], P(('dp', 'expert')), may hold values from -0.1875 to 0.1875
- depthwise: bfloat16 [1024, 31], P(('dp', 'expert')), may hold values from -1 to 1
- router: bfloat16 [1024, 64], P(('dp', 'expert')), may hold values from -0.1875 to 0.1875
- w_in: bfloat16 [64, 1024, 4096], P('expert', None, 'dp'), may hold values from -0.1875 to 0.1875
- w_out: bfloat16 [64, 4096, 1024], P('expert', 'dp'), may hold values from -0.09375 to 0.09375
- out_grad: bfloat16 [32768, 1024], P(('dp', 'expert')), may hold values from -6 to 6
Outputs:
- layer_out: bfloat16 [32768, 1024], P(('dp', 'expert'))
- frames_grad: bfloat16 [32768, 1024], P(('dp', 'expert'))
- conv_in_grad: float32 [1024, 2048], P(('dp', 'expert'))
- depthwise_grad: float32 [1024, 31], P(('dp', 'expert'))
- router_grad: float32 [1024, 64], P(('dp', 'expert'))
- w_in_grad: bfloat16 [64, 1024, 4096], P('expert', None, 'dp')
- w_out_grad: bfloat16 [64, 4096, 1024], P('expert', 'dp')
Inputs may be any that keep to these rules, and one draw needn't show every extreme that they name: `expert_ids`: each frame names 2 different experts, and every expert is named by some frame.
All inputs are finite; a program needn't handle non-finite values.
Results may differ from a plain program's by a relative error of at most 0.019.
Values may be sent and summed in bfloat16 or wider, within the bound.
A program may use at most 128 MiB of HBM per device.

v0:
```python
import jax
import jax.numpy as jnp
from jax import lax
from jax.sharding import PartitionSpec as P

TOP = 2
KERNEL = 31
EPSILON = 1e-05


def swish_of(values):
    return values * jax.nn.sigmoid(values)


def swish_slope(values):
    sigmoid_v = jax.nn.sigmoid(values)
    return sigmoid_v * (1.0 + values * (1.0 - sigmoid_v))


def normalize(values):
    center = values - jnp.mean(values, axis=-1, keepdims=True)
    inv_scale = lax.rsqrt(jnp.mean(center * center, axis=-1, keepdims=True) + EPSILON)
    return (center * inv_scale, inv_scale)


def norm_backward(upstream, centred, inv_scale):
    first_mean = jnp.mean(upstream, axis=-1, keepdims=True)
    second_mean = jnp.mean(upstream * centred, axis=-1, keepdims=True)
    return inv_scale * (upstream - first_mean - centred * second_mean)


def pad_time(signal, half_width):
    return jnp.pad(signal, ((half_width, half_width), (0, 0)))


def depth_apply(signal, tap_rows, half_width):
    length = signal.shape[0]
    padded = pad_time(signal, half_width)
    summed = jnp.zeros(signal.shape, jnp.float32)
    for tap_index in range(tap_rows.shape[0]):
        summed = summed + tap_rows[tap_index] * lax.slice_in_dim(
            padded, tap_index, tap_index + length, axis=0
        )
    return summed


def depth_transpose(upstream, tap_rows, half_width):
    length = upstream.shape[0]
    padded = pad_time(upstream, half_width)
    summed = jnp.zeros(upstream.shape, jnp.float32)
    for tap_index in range(tap_rows.shape[0]):
        begin = 2 * half_width - tap_index
        summed = summed + tap_rows[tap_index] * lax.slice_in_dim(
            padded, begin, begin + length, axis=0
        )
    return summed


def depth_taps_grad(upstream, signal, half_width):
    length = signal.shape[0]
    padded = pad_time(signal, half_width)
    rows_list = []
    for tap_index in range(2 * half_width + 1):
        piece = lax.slice_in_dim(padded, tap_index, tap_index + length, axis=0)
        rows_list.append(jnp.sum(upstream * piece, axis=0))
    return jnp.stack(rows_list, axis=0)


def routing(choices, length, experts, capacity):
    tokens, top_count = choices.shape
    usable = jnp.arange(tokens, dtype=jnp.int32) < length
    flat_ids = choices.reshape(-1)
    live = jnp.repeat(usable, top_count)
    onehot = (flat_ids[:, None] == jnp.arange(experts, dtype=jnp.int32)[None, :]) & live[:, None]
    onehot_int = onehot.astype(jnp.int32)
    before = jnp.cumsum(onehot_int, axis=0) - onehot_int
    position = jnp.sum(jnp.where(onehot, before, 0), axis=1)
    kept_rows = live & (position < capacity)
    slot_total = experts * capacity
    slot_index = jnp.where(kept_rows, flat_ids * capacity + position, slot_total)
    match = slot_index[None, :] == jnp.arange(slot_total, dtype=jnp.int32)[:, None]
    filled = jnp.any(match, axis=1)
    source = jnp.sum(
        jnp.where(match, jnp.arange(tokens * top_count, dtype=jnp.int32)[None, :], 0), axis=1
    )
    return (usable, kept_rows, jnp.minimum(slot_index, slot_total - 1), filled, source)


def dispatch(send_rows):
    arrived_cols = lax.all_to_all(send_rows, "expert", split_axis=0, concat_axis=0, tiled=True)
    arrived = lax.all_gather(arrived_cols[None], "dp", axis=0, tiled=True)
    return arrived.reshape(-1, send_rows.shape[-1])


def collect(term_maker, rows_here, columns, capacity, width):
    summed = lax.psum_scatter(
        term_maker(jnp.int32(0), rows_here * lax.axis_size("dp")).astype(jnp.bfloat16),
        "dp",
        scatter_dimension=0,
        tiled=True,
    )
    returned = lax.all_to_all(
        summed.reshape(columns, capacity, width), "expert", split_axis=0, concat_axis=0, tiled=True
    )
    return returned.reshape(columns * capacity, width)


def per_device(frames, lengths, expert_ids, conv_in, depthwise, router, w_in, w_out, out_grad):
    tokens, width = frames.shape
    experts = router.shape[1]
    capacity = TOP * tokens // experts
    columns = lax.axis_size("expert")
    rows_here = columns * capacity
    half_width = (KERNEL - 1) // 2
    conv_full, depth_full, router_full = (
        lax.all_gather(conv_in, ("dp", "expert"), axis=0, tiled=True),
        lax.all_gather(depthwise, ("dp", "expert"), axis=0, tiled=True),
        lax.all_gather(router, ("dp", "expert"), axis=0, tiled=True),
    )
    usable, kept_rows, slot_index, filled, source = routing(
        expert_ids, lengths[0], experts, capacity
    )
    frame_mask = usable.astype(jnp.float32)[:, None]
    frame_wide = frames.astype(jnp.float32)
    centred, inv_scale = normalize(frame_wide)
    normed = centred.astype(jnp.bfloat16)
    pointwise = jnp.dot(normed, conv_full, preferred_element_type=jnp.float32)
    value_half = pointwise[:, :width]
    gate_sig = jax.nn.sigmoid(pointwise[:, width:])
    gated = value_half * gate_sig * frame_mask
    tap_rows = depth_full.astype(jnp.float32).T
    conv_sum = depth_apply(gated, tap_rows, half_width)
    mixed_rows = (frame_wide + swish_of(conv_sum) * frame_mask).astype(jnp.bfloat16)
    logits = jnp.dot(mixed_rows, router_full, preferred_element_type=jnp.float32)
    onehots = (expert_ids[:, :, None] == jnp.arange(experts, dtype=jnp.int32)).astype(jnp.float32)
    chosen = jnp.sum(logits[:, None, :] * onehots, axis=-1)
    scores = jax.nn.sigmoid(chosen)
    score_sum = jnp.sum(scores, axis=-1, keepdims=True)
    weights = scores / score_sum
    kept_wide = kept_rows.reshape(tokens, TOP).astype(jnp.float32)
    send_rows = jnp.take(mixed_rows, source // TOP, axis=0)
    send_rows = jnp.where(filled[:, None], send_rows, jnp.zeros((), jnp.bfloat16)).reshape(
        experts, capacity, width
    )
    slot_rows = dispatch(send_rows)
    hidden = jnp.dot(slot_rows, w_in[0], preferred_element_type=jnp.float32)
    active = swish_of(hidden).astype(jnp.bfloat16)

    def forward_term(start, count):
        partial_rows = jnp.dot(active, w_out[0], preferred_element_type=jnp.float32).astype(
            jnp.bfloat16
        )
        return lax.optimization_barrier(partial_rows).astype(jnp.float32)

    expert_rows = collect(forward_term, rows_here, columns, capacity, width)
    picked = jnp.take(expert_rows, slot_index, axis=0).reshape(tokens, TOP, width)
    picked_wide = picked.astype(jnp.float32) * kept_wide[..., None]
    layer_out = (
        mixed_rows.astype(jnp.float32) + jnp.sum(weights[..., None] * picked_wide, axis=1)
    ).astype(jnp.bfloat16)
    conv_back, depth_back, router_back = (
        lax.all_gather(conv_in, ("dp", "expert"), axis=0, tiled=True),
        lax.all_gather(depthwise, ("dp", "expert"), axis=0, tiled=True),
        lax.all_gather(router, ("dp", "expert"), axis=0, tiled=True),
    )
    grad_wide = out_grad.astype(jnp.float32)
    weight_grad = jnp.sum(grad_wide[:, None, :] * picked_wide, axis=-1)
    mean_term = jnp.sum(weight_grad * weights, axis=-1, keepdims=True)
    chosen_grad = (weight_grad - mean_term) / score_sum * scores * (1.0 - scores)
    logit_grad = jnp.sum(chosen_grad[..., None] * onehots, axis=1).astype(jnp.bfloat16)
    router_part = lax.dot_general(
        mixed_rows, logit_grad, (((0,), (0,)), ((), ())), preferred_element_type=jnp.float32
    )
    router_term = lax.dot_general(
        logit_grad, router_back, (((1,), (1,)), ((), ())), preferred_element_type=jnp.float32
    )
    slot_cot = (
        ((weights * kept_wide)[..., None] * grad_wide[:, None, :])
        .astype(jnp.bfloat16)
        .reshape(tokens * TOP, width)
    )
    cot_send = jnp.take(slot_cot, source, axis=0)
    cot_send = jnp.where(filled[:, None], cot_send, jnp.zeros((), jnp.bfloat16)).reshape(
        experts, capacity, width
    )
    cot_rows = dispatch(cot_send)
    act_grad = lax.dot_general(
        cot_rows, w_out[0], (((1,), (1,)), ((), ())), preferred_element_type=jnp.float32
    )
    pre_grad = (act_grad * swish_slope(hidden)).astype(jnp.bfloat16)
    w_out_grad = lax.dot_general(
        active, cot_rows, (((0,), (0,)), ((), ())), preferred_element_type=jnp.float32
    ).astype(jnp.bfloat16)[None]
    w_in_grad = lax.dot_general(
        slot_rows, pre_grad, (((0,), (0,)), ((), ())), preferred_element_type=jnp.float32
    ).astype(jnp.bfloat16)[None]

    def backward_term(start, count):
        partial_rows = lax.dot_general(
            pre_grad, w_in[0], (((1,), (1,)), ((), ())), preferred_element_type=jnp.float32
        ).astype(jnp.bfloat16)
        return lax.optimization_barrier(partial_rows).astype(jnp.float32)

    back_rows = collect(backward_term, rows_here, columns, capacity, width)
    slot_grad = jnp.take(back_rows, slot_index, axis=0).reshape(tokens, TOP, width)
    slot_grad = slot_grad.astype(jnp.float32) * kept_wide[..., None]
    mixed_grad = grad_wide + jnp.sum(slot_grad, axis=1) + router_term
    conv_grad = mixed_grad * frame_mask * swish_slope(conv_sum)
    tap_back = depth_back.astype(jnp.float32).T
    glu_grad = depth_transpose(conv_grad, tap_back, half_width) * frame_mask
    taps_grad = depth_taps_grad(conv_grad, gated, half_width)
    value_grad = glu_grad * gate_sig
    gate_grad = glu_grad * value_half * gate_sig * (1.0 - gate_sig)
    pre_cot = jnp.concatenate([value_grad, gate_grad], axis=-1).astype(jnp.bfloat16)
    conv_part = lax.dot_general(
        normed, pre_cot, (((0,), (0,)), ((), ())), preferred_element_type=jnp.float32
    )
    normed_grad = lax.dot_general(
        pre_cot, conv_back, (((1,), (1,)), ((), ())), preferred_element_type=jnp.float32
    )
    frames_grad = (mixed_grad + norm_backward(normed_grad, centred, inv_scale)).astype(jnp.bfloat16)
    conv_in_grad, depthwise_grad, router_grad = (
        lax.psum_scatter(conv_part, ("dp", "expert"), scatter_dimension=0, tiled=True),
        lax.psum_scatter(taps_grad.T, ("dp", "expert"), scatter_dimension=0, tiled=True),
        lax.psum_scatter(router_part, ("dp", "expert"), scatter_dimension=0, tiled=True),
    )
    return (
        layer_out,
        frames_grad,
        conv_in_grad,
        depthwise_grad,
        router_grad,
        w_in_grad,
        w_out_grad,
    )


def solution(mesh):
    in_specs = (
        P(("dp", "expert"), None),
        P(("dp", "expert")),
        P(("dp", "expert"), None),
        P(("dp", "expert"), None),
        P(("dp", "expert"), None),
        P(("dp", "expert"), None),
        P("expert", None, "dp"),
        P("expert", "dp", None),
        P(("dp", "expert"), None),
    )
    out_specs = (
        P(("dp", "expert"), None),
        P(("dp", "expert"), None),
        P(("dp", "expert"), None),
        P(("dp", "expert"), None),
        P(("dp", "expert"), None),
        P("expert", None, "dp"),
        P("expert", "dp", None),
    )
    return jax.shard_map(
        per_device, mesh=mesh, in_specs=in_specs, out_specs=out_specs, check_vma=False
    )
```

profile of v0, /device:TPU:8, one launch (start us, length us, event | category | flops | bytes accessed | tf_op | source)
XLA Modules:
  0.0 790.0 jit_solution(2469328729457799150)
XLA Ops:
  11.9 65.2 %all-gather.2 = bf16[256,4,31]{2,1,0:T(4,128)(2,1)S(1)} all-gather(bf16[1,4,31]{2,1,0:T(4,128)(2,1)} %bitcast.231), channel_id=1, replica_groups=mesh['dp'=4,'expert'=64] {'dp','expert'}, dimensions={0}, use_global_device_ids=true | all-gather | bytes 63736 | tf_op jit(solution)/shard_map/all_gather | solution.py:117
  79.9 49.8 %all-gather.13.cloned.1.call-done = bf16[256,4,2048]{2,1,0:T(4,128)(2,1)} async-done(((bf16[1,4,2048]{2,1,0:T(4,128)(2,1)}), bf16[256,4,2048]{2,1,0:T(4,128)(2,1)}) %all-gather.13.cloned.1.call-update) | async-done | bytes 4194320 | tf_op jit(solution)/shard_map/all_gather | solution.py:116
  129.7 6.9 reshape.380
  147.5 24.6 %all_to_all.20 = bf16[64,4,1024]{2,1,0:T(4,128)(2,1)} all-to-all(bf16[64,4,1024]{2,1,0:T(4,128)(2,1)S(1)} %select_select_fusion.1), channel_id=1, replica_groups=mesh['dp'=4,'expert'=64] {'expert'}, dimensions={0} | all-to-all | bytes 1048576 | tf_op jit(solution)/shard_map/all_to_all | solution.py:90
  172.1 29.8 %all-gather.9.cloned.1.call-done = bf16[256,4,1024]{2,1,0:T(4,128)(2,1)} async-done(((bf16[64,4,1024]{2,1,0:T(4,128)(2,1)}), bf16[256,4,1024]{2,1,0:T(4,128)(2,1)}) %all-gather.9.cloned.1.call-update) | async-done | bytes 2097168 | tf_op jit(solution)/shard_map/all_gather | solution.py:91
  201.9 3.9 reshape.326
  205.8 4.5 fusion.5
  212.3 3.7 fusion.10
  216.1 32.4 %reduce-scatter.4.cloned.1.call-done = bf16[256,1024]{1,0:T(8,128)(2,1)} async-done(((bf16[1024,1024]{1,0:T(8,128)(2,1)}), bf16[256,1024]{1,0:T(8,128)(2,1)}) %reduce-scatter.4.cloned.1.call-update) | async-done | bytes 524304 | tf_op jit(solution)/shard_map/reduce_scatter | solution.py:96
  250.6 10.8 %all-to-all-start.1 = ((bf16[64,4,1024]{2,1,0:T(4,128)(2,1)}), bf16[64,4,1024]{2,1,0:T(4,128)(2,1)}, u32[]{:S(2)}, u32[]{:S(2)}) async-start(bf16[64,4,1024]{2,1,0:T(4,128)(2,1)} %reshape.327), calls=%async_computation.2 | async-start | bytes 1048576 | tf_op jit(solution)/shard_map/all_to_all | solution.py:102
  261.4 65.0 %all-gather.4 = bf16[256,4,64]{2,1,0:T(4,128)(2,1)S(1)} all-gather(bf16[1,4,64]{2,1,0:T(4,128)(2,1)S(1)} %bitcast.232), channel_id=1, replica_groups=mesh['dp'=4,'expert'=64] {'dp','expert'}, dimensions={0}, use_global_device_ids=true | all-gather | bytes 131584 | tf_op jit(solution)/shard_map/all_gather | solution.py:118
  342.3 25.9 %all_to_all.21 = bf16[64,4,1024]{2,1,0:T(4,128)(2,1)} all-to-all(bf16[64,4,1024]{2,1,0:T(4,128)(2,1)} %reshape.330), channel_id=1, replica_groups=mesh['dp'=4,'expert'=64] {'expert'}, dimensions={0} | all-to-all | bytes 1048576 | tf_op jit(solution)/shard_map/all_to_all | solution.py:90
  368.3 30.5 %all-gather.11.cloned.1.call-done = bf16[256,4,1024]{2,1,0:T(4,128)(2,1)} async-done(((bf16[64,4,1024]{2,1,0:T(4,128)(2,1)}), bf16[256,4,1024]{2,1,0:T(4,128)(2,1)}) %all-gather.11.cloned.1.call-update) | async-done | bytes 2097168 | tf_op jit(solution)/shard_map/all_gather | solution.py:91
  398.8 4.0 reshape.331
  402.8 6.1 multiply_convert_fusion
  410.2 3.7 fusion.7
  413.9 32.4 %reduce-scatter.6.cloned.1.call-done = bf16[256,1024]{1,0:T(8,128)(2,1)} async-done(((bf16[1024,1024]{1,0:T(8,128)(2,1)}), bf16[256,1024]{1,0:T(8,128)(2,1)}) %reduce-scatter.6.cloned.1.call-update) | async-done | bytes 524304 | tf_op jit(solution)/shard_map/reduce_scatter | solution.py:96
  448.4 10.6 %all-to-all-start.3 = ((bf16[64,4,1024]{2,1,0:T(4,128)(2,1)}), bf16[64,4,1024]{2,1,0:T(4,128)(2,1)S(1)}, u32[]{:S(2)}, u32[]{:S(2)}) async-start(bf16[64,4,1024]{2,1,0:T(4,128)(2,1)} %reshape.332), calls=%async_computation.5 | async-start | bytes 1048576 | tf_op jit(solution)/shard_map/all_to_all | solution.py:102
  460.4 15.3 %all-to-all-done.3 = bf16[64,4,1024]{2,1,0:T(4,128)(2,1)S(1)} async-done(((bf16[64,4,1024]{2,1,0:T(4,128)(2,1)}), bf16[64,4,1024]{2,1,0:T(4,128)(2,1)S(1)}, u32[]{:S(2)}, u32[]{:S(2)}) %all-to-all-start.3) | async-done | bytes 524320 | tf_op jit(solution)/shard_map/all_to_all | solution.py:102
  482.5 5.0 multiply_reduce_fusion.1
  494.6 4.6 fusion.89
  503.6 5.5 convert_bitcast_fusion.1
  509.0 3.8 convert_bitcast_fusion
  516.2 262.3 %all-reduce.8.cloned.1.call-done = (f32[1024,2048]{1,0:T(8,128)}, f32[1024,31]{0,1:T(8,128)}, f32[1024,64]{1,0:T(8,128)}) async-done(((f32[1024,2048]{1,0:T(8,128)}, f32[1024,31]{0,1:T(8,128)}, f32[1024,64]{1,0:T(8,128)}), (f32[1024,2048]{1,0:T(8,128)}, f32[1024,31]{0,1:T(8,128)}, f32[1024,64]{1,0:T(8,128)})) %all-reduce.8.cloned.1.call-update) | async-done | bytes 8777744
  (323 shorter events, 66.9 us)
Async XLA Ops:
  7.2 205.2 %copy-start = (bf16[1,1024,1024]{2,1,0:T(8,128)(2,1)S(1)}, bf16[1,1024,1024]{2,1,0:T(8,128)(2,1)}, u32[]{:S(2)}) copy-start(bf16[1,1024,1024]{2,1,0:T(8,128)(2,1)} %param.18) | copy-start | bytes 6291460
  7.2 122.5 %all-gather.13.cloned.1.call-start = ((), (), s32[]{:S(2)}) async-start(), calls=%async_computation.10 | async-start | bytes 4210688 | tf_op jit(solution)/shard_map/all_gather | solution.py:116
  7.9 193.9 %all-gather.9.cloned.1.call-start = ((), (), s32[]{:S(2)}) async-start(), calls=%async_computation.8 | async-start | bytes 2621440 | tf_op jit(solution)/shard_map/all_gather | solution.py:91
  11.2 322.9 %copy-start.87 = (pred[256]{0:T(512)(128)(4,1)}, pred[256]{0:T(512)(128)(4,1)S(1)}, u32[]{:S(2)}) copy-start(pred[256]{0:T(512)(128)(4,1)S(1)} %get-tuple-element.81) | copy-start | bytes 772
  77.2 63.4 %copy-start.85 = (f32[128]{0:T(128)}, f32[128]{0:T(128)S(1)}, u32[]{:S(2)}) copy-start(f32[128]{0:T(128)S(1)} %fusion.106) | copy-start | bytes 1540
  79.6 61.0 %copy-start.16 = (f32[1,1024]{1,0:T(1,128)}, f32[1,1024]{1,0:T(1,128)S(1)}, u32[]{:S(2)}) copy-start(f32[1,1024]{1,0:T(1,128)S(1)} %get-tuple-element.106) | copy-start | bytes 12292
  79.6 61.0 %copy-start.18 = (f32[1,1024]{1,0:T(1,128)}, f32[1,1024]{1,0:T(1,128)S(1)}, u32[]{:S(2)}) copy-start(f32[1,1024]{1,0:T(1,128)S(1)} %get-tuple-element.107) | copy-start | bytes 12292
  79.6 61.0 %copy-start.20 = (f32[1,1024]{1,0:T(1,128)}, f32[1,1024]{1,0:T(1,128)S(1)}, u32[]{:S(2)}) copy-start(f32[1,1024]{1,0:T(1,128)S(1)} %get-tuple-element.108) | copy-start | bytes 12292
  79.6 61.0 %copy-start.22 = (f32[1,1024]{1,0:T(1,128)}, f32[1,1024]{1,0:T(1,128)S(1)}, u32[]{:S(2)}) copy-start(f32[1,1024]{1,0:T(1,128)S(1)} %get-tuple-element.109) | copy-start | bytes 12292
  79.6 61.0 %copy-start.24 = (f32[1,1024]{1,0:T(1,128)}, f32[1,1024]{1,0:T(1,128)S(1)}, u32[]{:S(2)}) copy-start(f32[1,1024]{1,0:T(1,128)S(1)} %get-tuple-element.110) | copy-start | bytes 12292
  79.6 61.0 %copy-start.26 = (f32[1,1024]{1,0:T(1,128)}, f32[1,1024]{1,0:T(1,128)S(1)}, u32[]{:S(2)}) copy-start(f32[1,1024]{1,0:T(1,128)S(1)} %get-tuple-element.111) | copy-start | bytes 12292
  79.6 61.0 %copy-start.28 = (f32[1,1024]{1,0:T(1,128)}, f32[1,1024]{1,0:T(1,128)S(1)}, u32[]{:S(2)}) copy-start(f32[1,1024]{1,0:T(1,128)S(1)} %get-tuple-element.112) | copy-start | bytes 12292
  79.6 61.0 %copy-start.30 = (f32[1,1024]{1,0:T(1,128)}, f32[1,1024]{1,0:T(1,128)S(1)}, u32[]{:S(2)}) copy-start(f32[1,1024]{1,0:T(1,128)S(1)} %get-tuple-element.113) | copy-start | bytes 12292
  79.6 61.0 %copy-start.32 = (f32[1,1024]{1,0:T(1,128)}, f32[1,1024]{1,0:T(1,128)S(1)}, u32[]{:S(2)}) copy-start(f32[1,1024]{1,0:T(1,128)S(1)} %get-tuple-element.114) | copy-start | bytes 12292
  79.7 61.0 %copy-start.34 = (f32[1,1024]{1,0:T(1,128)}, f32[1,1024]{1,0:T(1,128)S(1)}, u32[]{:S(2)}) copy-start(f32[1,1024]{1,0:T(1,128)S(1)} %get-tuple-element.115) | copy-start | bytes 12292
  172.0 76.5 %reduce-scatter.4.cloned.1.call-start = ((), (), s32[]{:S(2)}) async-start(), calls=%async_computation.6 | async-start | bytes 2621440 | tf_op jit(solution)/shard_map/reduce_scatter | solution.py:96
  216.0 110.4 %copy-start.14 = (bf16[128,1024]{1,0:T(8,128)(2,1)S(1)}, bf16[128,1024]{1,0:T(8,128)(2,1)}, u32[]{:S(2)}) copy-start(bf16[128,1024]{1,0:T(8,128)(2,1)} %param.19) | copy-start | bytes 786436
  250.6 80.4 %all-to-all-start.1 = ((bf16[64,4,1024]{2,1,0:T(4,128)(2,1)}), bf16[64,4,1024]{2,1,0:T(4,128)(2,1)}, u32[]{:S(2)}, u32[]{:S(2)}) async-start(bf16[64,4,1024]{2,1,0:T(4,128)(2,1)} %reshape.327), calls=%async_computation.2 | async-start | bytes 1048576 | tf_op jit(solution)/shard_map/all_to_all | solution.py:102
  261.3 137.5 %all-gather.11.cloned.1.call-start = ((), (), s32[]{:S(2)}) async-start(), calls=%async_computation.9 | async-start | bytes 2621440 | tf_op jit(solution)/shard_map/all_gather | solution.py:91
  261.4 69.5 %copy-start.82 = (s32[128,2]{0,1:T(2,128)S(1)}, s32[128,2]{0,1:T(2,128)}, u32[]{:S(2)}) copy-start(s32[128,2]{0,1:T(2,128)} %param.13) | copy-start | bytes 3076
  368.2 78.1 %reduce-scatter.6.cloned.1.call-start = ((), (), s32[]{:S(2)}) async-start(), calls=%async_computation.7 | async-start | bytes 2621440 | tf_op jit(solution)/shard_map/reduce_scatter | solution.py:96
  448.4 27.3 %all-to-all-start.3 = ((bf16[64,4,1024]{2,1,0:T(4,128)(2,1)}), bf16[64,4,1024]{2,1,0:T(4,128)(2,1)S(1)}, u32[]{:S(2)}, u32[]{:S(2)}) async-start(bf16[64,4,1024]{2,1,0:T(4,128)(2,1)} %reshape.332), calls=%async_computation.5 | async-start | bytes 1048576 | tf_op jit(solution)/shard_map/all_to_all | solution.py:102
  459.0 319.6 %all-reduce.8.cloned.1.call-start = ((), (), s32[]{:S(2)}) async-start(), calls=%async_computation.11 | async-start | bytes 18087936
  512.9 269.9 %copy-start.1 = (bf16[1,1024,1024]{2,1,0:T(8,128)(2,1)S(1)}, bf16[1,1024,1024]{2,1,0:T(8,128)(2,1)}, u32[]{:S(2)}) copy-start(bf16[1,1024,1024]{2,1,0:T(8,128)(2,1)} %param.18) | copy-start | bytes 6291460
  (95 other events, 1864.5 us)
Sparse Core Ops, SparseCore 0:
  11.7 117.9 all-gather.12
  172.2 29.6 all-gather.8
  216.2 32.2 reduce-scatter.3
  368.4 30.4 all-gather.10
  414.1 32.2 reduce-scatter.5
  502.1 276.3 all-reduce.7
where the time goes:
time: 800 us; the launch traced here: 790 us
  waiting for transfers between devices  453 us (57%)
  blocking collectives  181 us (23%)
  local copies, waits for them, and re-layouts  52.2 us (7%)
  matrix products  40.9 us (5%)
  other arithmetic  24.6 us (3%)
  starting transfers between devices  21.6 us (3%)
  between operations  16.9 us (2%)
    unnamed x7, waiting for transfers between devices  263 us
    all_gather x1, blocking collectives, per_device(): lax.all_gather(depthwise, ('dp', 'expert'), axis=0, tiled=True)  65.2 us
    all_gather x1, blocking collectives, per_device(): lax.all_gather(router, ('dp', 'expert'), axis=0, tiled=True)  65 us
    reduce_scatter x2, waiting for transfers between devices, collect(): lax.psum_scatter(term_maker(jnp.int32(0), rows_here * lax.axis_size('dp')...  64.8 us
    all_gather x2, waiting for transfers between devices, dispatch(): arrived = lax.all_gather(arrived_cols[None], 'dp', axis=0, tiled=True)  60.3 us
    all_to_all x2, blocking collectives, dispatch(): lax.all_to_all(send_rows, 'expert', split_axis=0, concat_axis=0, tiled=True)  50.5 us
    all_gather x1, waiting for transfers between devices, per_device(): lax.all_gather(conv_in, ('dp', 'expert'), axis=0, tiled=True)  49.8 us
    all_to_all x2, starting transfers between devices, collect(): lax.all_to_all(summed.reshape(columns, capacity, width), 'expert', split_...  21.3 us
  transfers between devices with their start and end apart: 8, of which 7 were waited for; matrix products, arithmetic and copies ran while one was open for 3% of the time, Pallas kernels for 0%

commit v1 on v0

--- a/solution.py
+++ b/solution.py
@@ -114,7 +114,12 @@
     half_width = (KERNEL - 1) // 2
     conv_full, depth_full, router_full = (
         lax.all_gather(conv_in, ("dp", "expert"), axis=0, tiled=True),
-        lax.all_gather(depthwise, ("dp", "expert"), axis=0, tiled=True),
+        jnp.concatenate(
+            lax.all_to_all(
+                jnp.stack([depthwise] * lax.axis_size(("dp", "expert"))), ("dp", "expert"), 0, 0
+            ),
+            axis=0,
+        ),
         lax.all_gather(router, ("dp", "expert"), axis=0, tiled=True),
     )
     usable, kept_rows, slot_index, filled, source = routing(

time: 800 us -> 829 us (1.036)
  starting transfers between devices: 21.6 us -> 34 us
  local copies, waits for them, and re-layouts: 52.2 us -> 63.8 us
    all_gather x1, waiting for transfers between devices: 49.8 us -> 82.2 us  [per_device(): lax.all_gather(conv_in, ('dp', 'expert'), axis=0, tiled=True)]
    reduce_scatter x2, waiting for transfers between devices: 64.8 us -> 32.4 us  [collect(): lax.psum_scatter(term_maker(jnp.int32(0), rows_here * lax.axis_size('dp')...]
    all_to_all x0 -> x1, starting transfers between devices: none -> 14.6 us  [per_device(): lax.all_to_all(jnp.stack([depthwise] * lax.axis_size(('dp', 'expert'))),...]
    all_to_all x0 -> x1, waiting for transfers between devices: none -> 8.75 us  [per_device(): lax.all_to_all(jnp.stack([depthwise] * lax.axis_size(('dp', 'expert'))),...]
    slice x2, local copies, waits for them, and re-layouts: 0.1 us -> 8.43 us  [depth_apply(): tap_rows[tap_index]]
    unnamed x228 -> x168, local copies, waits for them, and re-layouts: 17.9 us -> 18.5 us
  transfers between devices with their start and end apart: 8 -> 9, of which waited for: 7 -> 7; matrix products, arithmetic and copies ran while one was open for 3% -> 4% of each run, Pallas kernels for 0% -> 0%
where the time goes in v1:
time: 829 us; the launch traced here: 818 us
  waiting for transfers between devices  461 us (56%)
  blocking collectives  177 us (21%)
  local copies, waits for them, and re-layouts  63.8 us (8%)
  matrix products  41.1 us (5%)
  starting transfers between devices  34 us (4%)
  other arithmetic  24.5 us (3%)
  between operations  16.4 us (2%)
    unnamed x7, waiting for transfers between devices  264 us
    all_gather x1, waiting for transfers between devices, per_device(): lax.all_gather(conv_in, ('dp', 'expert'), axis=0, tiled=True)  82.2 us
    all_gather x1, blocking collectives, per_device(): lax.all_gather(router, ('dp', 'expert'), axis=0, tiled=True)  65 us
    all_gather x1, blocking collectives, per_device(): lax.all_gather(depthwise, ('dp', 'expert'), axis=0, tiled=True)  61 us
    all_gather x2, waiting for transfers between devices, dispatch(): arrived = lax.all_gather(arrived_cols[None], 'dp', axis=0, tiled=True)  60.1 us
    all_to_all x2, blocking collectives, dispatch(): lax.all_to_all(send_rows, 'expert', split_axis=0, concat_axis=0, tiled=True)  50.8 us
    reduce_scatter x2, waiting for transfers between devices, collect(): lax.psum_scatter(term_maker(jnp.int32(0), rows_here * lax.axis_size('dp')...  32.4 us
    all_to_all x2, starting transfers between devices, collect(): lax.all_to_all(summed.reshape(columns, capacity, width), 'expert', split_...  19 us
  transfers between devices with their start and end apart: 9, of which 7 were waited for; matrix products, arithmetic and copies ran while one was open for 4% of the time, Pallas kernels for 0%

profile of v1, /device:TPU:8, one launch (start us, length us, event | category | flops | bytes accessed | tf_op | source)
XLA Modules:
  0.0 818.2 jit_solution(10453811116927901489)
XLA Ops:
  9.4 14.6 %all-to-all-start = ((bf16[256,4,31]{2,1,0:T(4,128)(2,1)}), bf16[256,4,31]{2,1,0:T(4,128)(2,1)S(1)}, u32[]{:S(2)}, u32[]{:S(2)}) async-start(bf16[256,4,31]{2,1,0:T(4,128)(2,1)} %stack.66), calls=%async_computation | async-start | bytes 524288 | tf_op jit(solution)/shard_map/all_to_all | solution.py:118
  30.3 8.8 %all-to-all-done = bf16[256,4,31]{2,1,0:T(4,128)(2,1)S(1)} async-done(((bf16[256,4,31]{2,1,0:T(4,128)(2,1)}), bf16[256,4,31]{2,1,0:T(4,128)(2,1)S(1)}, u32[]{:S(2)}, u32[]{:S(2)}) %all-to-all-start) | async-done | bytes 63520 | tf_op jit(solution)/shard_map/all_to_all | solution.py:118
  42.4 5.1 slice_reduce_fusion.30
  47.5 82.2 %all-gather.13.cloned.1.call-done = bf16[256,4,2048]{2,1,0:T(4,128)(2,1)} async-done(((bf16[1,4,2048]{2,1,0:T(4,128)(2,1)}), bf16[256,4,2048]{2,1,0:T(4,128)(2,1)}) %all-gather.13.cloned.1.call-update) | async-done | bytes 4194320 | tf_op jit(solution)/shard_map/all_gather | solution.py:116
  129.8 6.9 reshape.384
  147.3 24.9 %all_to_all.25 = bf16[64,4,1024]{2,1,0:T(4,128)(2,1)} all-to-all(bf16[64,4,1024]{2,1,0:T(4,128)(2,1)S(1)} %select_select_fusion.1), channel_id=1, replica_groups=mesh['dp'=4,'expert'=64] {'expert'}, dimensions={0} | all-to-all | bytes 1048576 | tf_op jit(solution)/shard_map/all_to_all | solution.py:90
  172.3 29.8 %all-gather.9.cloned.1.call-done = bf16[256,4,1024]{2,1,0:T(4,128)(2,1)} async-done(((bf16[64,4,1024]{2,1,0:T(4,128)(2,1)}), bf16[256,4,1024]{2,1,0:T(4,128)(2,1)}) %all-gather.9.cloned.1.call-update) | async-done | bytes 2097168 | tf_op jit(solution)/shard_map/all_gather | solution.py:91
  202.0 3.9 reshape.331
  206.0 4.5 fusion.5
  216.3 32.4 %reduce-scatter.4.cloned.1.call-done = bf16[256,1024]{1,0:T(8,128)(2,1)} async-done(((bf16[1024,1024]{1,0:T(8,128)(2,1)}), bf16[256,1024]{1,0:T(8,128)(2,1)}) %reduce-scatter.4.cloned.1.call-update) | async-done | bytes 524304 | tf_op jit(solution)/shard_map/reduce_scatter | solution.py:96
  250.7 10.8 %all-to-all-start.2 = ((bf16[64,4,1024]{2,1,0:T(4,128)(2,1)}), bf16[64,4,1024]{2,1,0:T(4,128)(2,1)}, u32[]{:S(2)}, u32[]{:S(2)}) async-start(bf16[64,4,1024]{2,1,0:T(4,128)(2,1)} %reshape.332), calls=%async_computation.3 | async-start | bytes 1048576 | tf_op jit(solution)/shard_map/all_to_all | solution.py:102
  261.5 65.0 %all-gather.3 = bf16[256,4,64]{2,1,0:T(4,128)(2,1)S(1)} all-gather(bf16[1,4,64]{2,1,0:T(4,128)(2,1)S(1)} %bitcast.206), channel_id=1, replica_groups=mesh['dp'=4,'expert'=64] {'dp','expert'}, dimensions={0}, use_global_device_ids=true | all-gather | bytes 131584 | tf_op jit(solution)/shard_map/all_gather | solution.py:123
  342.4 25.9 %all_to_all.26 = bf16[64,4,1024]{2,1,0:T(4,128)(2,1)} all-to-all(bf16[64,4,1024]{2,1,0:T(4,128)(2,1)} %reshape.335), channel_id=1, replica_groups=mesh['dp'=4,'expert'=64] {'expert'}, dimensions={0} | all-to-all | bytes 1048576 | tf_op jit(solution)/shard_map/all_to_all | solution.py:90
  368.6 30.3 %all-gather.11.cloned.1.call-done = bf16[256,4,1024]{2,1,0:T(4,128)(2,1)} async-done(((bf16[64,4,1024]{2,1,0:T(4,128)(2,1)}), bf16[256,4,1024]{2,1,0:T(4,128)(2,1)}) %all-gather.11.cloned.1.call-update) | async-done | bytes 2097168 | tf_op jit(solution)/shard_map/all_gather | solution.py:91
  399.0 4.0 reshape.336
  403.0 6.1 multiply_convert_fusion
  414.7 61.0 %all-gather.4 = bf16[256,4,31]{2,1,0:T(4,128)(2,1)S(1)} all-gather(bf16[1,4,31]{2,1,0:T(4,128)(2,1)S(1)} %bitcast.204), channel_id=1, replica_groups=mesh['dp'=4,'expert'=64] {'dp','expert'}, dimensions={0}, use_global_device_ids=true | all-gather | bytes 63736 | tf_op jit(solution)/shard_map/all_gather | solution.py:168
  478.0 8.2 %all-to-all-start.4 = ((bf16[64,4,1024]{2,1,0:T(4,128)(2,1)}), bf16[64,4,1024]{2,1,0:T(4,128)(2,1)S(1)}, u32[]{:S(2)}, u32[]{:S(2)}) async-start(bf16[64,4,1024]{2,1,0:T(4,128)(2,1)} %reshape.337), calls=%async_computation.6 | async-start | bytes 1048576 | tf_op jit(solution)/shard_map/all_to_all | solution.py:102
  488.8 14.1 %all-to-all-done.4 = bf16[64,4,1024]{2,1,0:T(4,128)(2,1)S(1)} async-done(((bf16[64,4,1024]{2,1,0:T(4,128)(2,1)}), bf16[64,4,1024]{2,1,0:T(4,128)(2,1)S(1)}, u32[]{:S(2)}, u32[]{:S(2)}) %all-to-all-start.4) | async-done | bytes 524320 | tf_op jit(solution)/shard_map/all_to_all | solution.py:102
  509.8 5.0 multiply_reduce_fusion.1
  522.2 4.6 fusion.89
  531.1 5.4 convert_bitcast_fusion.1
  536.6 3.8 convert_bitcast_fusion
  543.7 263.0 %all-reduce.8.cloned.1.call-done = (f32[1024,2048]{1,0:T(8,128)}, f32[1024,31]{0,1:T(8,128)}, f32[1024,64]{1,0:T(8,128)}) async-done(((f32[1024,2048]{1,0:T(8,128)}, f32[1024,31]{0,1:T(8,128)}, f32[1024,64]{1,0:T(8,128)}), (f32[1024,2048]{1,0:T(8,128)}, f32[1024,31]{0,1:T(8,128)}, f32[1024,64]{1,0:T(8,128)})) %all-reduce.8.cloned.1.call-update) | async-done | bytes 8777744
  (269 shorter events, 81.2 us)
Async XLA Ops:
  7.2 205.3 %copy-start = (bf16[1,1024,1024]{2,1,0:T(8,128)(2,1)S(1)}, bf16[1,1024,1024]{2,1,0:T(8,128)(2,1)}, u32[]{:S(2)}) copy-start(bf16[1,1024,1024]{2,1,0:T(8,128)(2,1)} %param.18) | copy-start | bytes 6291460
  7.2 122.6 %all-gather.13.cloned.1.call-start = ((), (), s32[]{:S(2)}) async-start(), calls=%async_computation.11 | async-start | bytes 4210688 | tf_op jit(solution)/shard_map/all_gather | solution.py:116
  9.4 29.7 %all-to-all-start = ((bf16[256,4,31]{2,1,0:T(4,128)(2,1)}), bf16[256,4,31]{2,1,0:T(4,128)(2,1)S(1)}, u32[]{:S(2)}, u32[]{:S(2)}) async-start(bf16[256,4,31]{2,1,0:T(4,128)(2,1)} %stack.66), calls=%async_computation | async-start | bytes 524288 | tf_op jit(solution)/shard_map/all_to_all | solution.py:118
  24.0 178.1 %all-gather.9.cloned.1.call-start = ((), (), s32[]{:S(2)}) async-start(), calls=%async_computation.9 | async-start | bytes 2621440 | tf_op jit(solution)/shard_map/all_gather | solution.py:91
  27.3 307.0 %copy-start.56 = (pred[256]{0:T(512)(128)(4,1)}, pred[256]{0:T(512)(128)(4,1)S(1)}, u32[]{:S(2)}) copy-start(pred[256]{0:T(512)(128)(4,1)S(1)} %get-tuple-element.119) | copy-start | bytes 772
  28.8 107.9 %copy-start.16 = (f32[128]{0:T(128)}, f32[128]{0:T(128)S(1)}, u32[]{:S(2)}) copy-start(f32[128]{0:T(128)S(1)} %broadcast_multiply_fusion.2) | copy-start | bytes 1540
  30.0 106.7 %copy-start.49 = (f32[128]{0:T(128)}, f32[128]{0:T(128)S(1)}, u32[]{:S(2)}) copy-start(f32[128]{0:T(128)S(1)} %add_rsqrt_fusion) | copy-start | bytes 1540
  30.0 110.6 %copy-start.54 = (f32[128]{0:T(128)}, f32[128]{0:T(128)S(1)}, u32[]{:S(2)}) copy-start(f32[128]{0:T(128)S(1)} %fusion.106) | copy-start | bytes 1540
  47.5 89.2 %copy-start.3 = (bf16[128,1024]{1,0:T(8,128)(2,1)S(1)}, bf16[128,1024]{1,0:T(8,128)(2,1)}, u32[]{:S(2)}) copy-start(bf16[128,1024]{1,0:T(8,128)(2,1)} %param.11) | copy-start | bytes 786436
  172.2 76.5 %reduce-scatter.4.cloned.1.call-start = ((), (), s32[]{:S(2)}) async-start(), calls=%async_computation.7 | async-start | bytes 2621440 | tf_op jit(solution)/shard_map/reduce_scatter | solution.py:96
  216.2 45.3 %copy-start.76 = (bf16[4,64]{1,0:T(4,128)(2,1)S(1)}, bf16[4,64]{1,0:T(4,128)(2,1)}, u32[]{:S(2)}) copy-start(bf16[4,64]{1,0:T(4,128)(2,1)} %param.16) | copy-start | bytes 1540
  216.2 110.3 %copy-start.14 = (bf16[128,1024]{1,0:T(8,128)(2,1)S(1)}, bf16[128,1024]{1,0:T(8,128)(2,1)}, u32[]{:S(2)}) copy-start(bf16[128,1024]{1,0:T(8,128)(2,1)} %param.19) | copy-start | bytes 786436
  250.7 80.4 %all-to-all-start.2 = ((bf16[64,4,1024]{2,1,0:T(4,128)(2,1)}), bf16[64,4,1024]{2,1,0:T(4,128)(2,1)}, u32[]{:S(2)}, u32[]{:S(2)}) async-start(bf16[64,4,1024]{2,1,0:T(4,128)(2,1)} %reshape.332), calls=%async_computation.3 | async-start | bytes 1048576 | tf_op jit(solution)/shard_map/all_to_all | solution.py:102
  261.5 137.5 %all-gather.11.cloned.1.call-start = ((), (), s32[]{:S(2)}) async-start(), calls=%async_computation.10 | async-start | bytes 2621440 | tf_op jit(solution)/shard_map/all_gather | solution.py:91
  261.5 69.5 %copy-start.51 = (s32[128,2]{0,1:T(2,128)S(1)}, s32[128,2]{0,1:T(2,128)}, u32[]{:S(2)}) copy-start(s32[128,2]{0,1:T(2,128)} %param.13) | copy-start | bytes 3076
  368.4 107.6 %reduce-scatter.6.cloned.1.call-start = ((), (), s32[]{:S(2)}) async-start(), calls=%async_computation.8 | async-start | bytes 2621440 | tf_op jit(solution)/shard_map/reduce_scatter | solution.py:96
  403.0 7.4 copy-start.77
  414.1 73.6 %copy-start.75 = (f32[128]{0:T(128)S(1)}, f32[128]{0:T(128)}, u32[]{:S(2)}) copy-start(f32[128]{0:T(128)} %get-tuple-element.115) | copy-start | bytes 1540
  414.1 73.6 %copy-start.52 = (s32[128,2]{0,1:T(2,128)S(1)}, s32[128,2]{0,1:T(2,128)}, u32[]{:S(2)}) copy-start(s32[128,2]{0,1:T(2,128)} %param.13) | copy-start | bytes 3076
  478.0 24.9 %all-to-all-start.4 = ((bf16[64,4,1024]{2,1,0:T(4,128)(2,1)}), bf16[64,4,1024]{2,1,0:T(4,128)(2,1)S(1)}, u32[]{:S(2)}, u32[]{:S(2)}) async-start(bf16[64,4,1024]{2,1,0:T(4,128)(2,1)} %reshape.337), calls=%async_computation.6 | async-start | bytes 1048576 | tf_op jit(solution)/shard_map/all_to_all | solution.py:102
  486.3 320.5 %all-reduce.8.cloned.1.call-start = ((), (), s32[]{:S(2)}) async-start(), calls=%async_computation.12 | async-start | bytes 18087936
  531.1 5.5 copy-start.11
  531.1 5.5 copy-start.79
  540.4 270.6 %copy-start.1 = (bf16[1,1024,1024]{2,1,0:T(8,128)(2,1)S(1)}, bf16[1,1024,1024]{2,1,0:T(8,128)(2,1)}, u32[]{:S(2)}) copy-start(bf16[1,1024,1024]{2,1,0:T(8,128)(2,1)} %param.18) | copy-start | bytes 6291460
  (66 other events, 266.9 us)
Sparse Core Ops, SparseCore 0:
  11.7 117.9 all-gather.12
  172.3 29.6 all-gather.8
  216.4 32.2 reduce-scatter.3
  368.5 30.4 all-gather.10
  414.2 32.3 reduce-scatter.5
  529.7 277.0 all-reduce.7
